TPU v7x, 32 devices: a whole 2x2x4 slice. The times are simulated.
32 devices in a mesh: row: 16 (over z, y, x), col: 2 (over core).
Axes of the slice: x: 2, y: 2, z: 4, core: 2. Of those that a mesh axis runs over, the one named last changes fastest.
Arguments:
- acts: bfloat16 [2048, 8192], P('row'), may hold values from -22 to 22
- out_grads: bfloat16 [2048, 4096], P('row', 'col'), may hold values from -0.198873782 to 0.198873782
- weight: float32 [8192, 4096], P('row', 'col'), may hold values from -30 to 30
- row_state: float32 [8192], P('row'), may hold values from 0.002 to 2
- col_state: float32 [4096], P('col'), may hold values from 0.01 to 0.3
Outputs:
- new_weight: float32 [8192, 4096], P('row', 'col')
- update: float32 [8192, 4096], P('row', 'col')
- row_moment: float32 [8192], P('row')
- col_moment: float32 [4096], P('col')
All inputs are finite; a program needn't handle non-finite values.
Results may differ from a plain program's by a relative error of at most 0.0003.
Values may be sent and summed in bfloat16 or wider, within the bound.
No kernel may reach another device: no remote copies, remote signals or barrier semaphores. Data moves between devices by JAX's collectives and lax.ppermute only.
A program may use at most 64 MiB of HBM per device.

v0:
```python
import jax
import jax.numpy as jnp
from jax import lax
from jax.sharding import PartitionSpec as P

decay_rate = 0.85
floor_eps = 1e-30
relative_rate = 0.05


def per_device(acts, out_grads, weight, row_state, col_state):
    n_col = lax.axis_size("col")
    width = acts.shape[1]
    cols_here = out_grads.shape[1]
    cols_all = cols_here * n_col
    columns = lax.all_to_all(acts, "row", split_axis=1, concat_axis=0, tiled=True)
    gradient = lax.dot_general(
        columns,
        lax.all_gather(out_grads, "row", axis=0, tiled=True),
        (((0,), (0,)), ((), ())),
        preferred_element_type=jnp.float32,
    )
    squares = gradient * gradient + floor_eps
    row_squares = jnp.sum(squares, axis=1)
    col_squares = jnp.sum(squares, axis=0)
    weight_part = jnp.sum(weight * weight)
    row_total = lax.psum(row_squares, "col")
    col_total = lax.psum(col_squares, "row")
    weight_total = lax.psum(weight_part, ("row", "col"))
    row_moment = decay_rate * row_state + (1.0 - decay_rate) * (row_total / cols_all)
    col_moment = decay_rate * col_state + (1.0 - decay_rate) * (col_total / width)
    unclipped = gradient * lax.rsqrt(row_moment[:, None] * col_moment[None, :])
    update_total = lax.psum(jnp.sum(unclipped * unclipped), ("row", "col"))
    count_all = width * cols_all
    clip_factor = jnp.maximum(1.0, jnp.sqrt(update_total / count_all))
    update = unclipped / clip_factor
    step_size = relative_rate * jnp.sqrt(weight_total / count_all + 1e-06)
    new_weight = weight - step_size * update
    return (new_weight, update, row_moment, col_moment)


def solution(mesh):
    return jax.shard_map(
        per_device,
        mesh=mesh,
        in_specs=(P("row", None), P("row", "col"), P("row", "col"), P("row"), P("col")),
        out_specs=(P("row", "col"), P("row", "col"), P("row"), P("col")),
        check_vma=False,
    )
```

profile of v0, /device:TPU:12, one launch (start us, length us, event | category | flops | bytes accessed | tf_op | source)
XLA Modules:
  0.0 269.7 jit_solution(2994545322753481755)
XLA Ops:
  7.2 0.0 all-gather.2.cloned.1.call-start
  7.2 0.7 all-gather.2.cloned.1.call-update
  7.9 4.1 %copy.9 = bf16[128,8192]{0,1:T(8,128)(2,1)} copy(bf16[128,8192]{1,0:T(8,128)(2,1)} %param.5) | data formatting | bytes 4194304 | tf_op args[0]
  12.0 7.2 %all-to-all-start = ((bf16[128,16,512]{0,2,1:T(8,128)(2,1)}), bf16[128,16,512]{0,2,1:T(8,128)(2,1)S(1)}, u32[]{:S(2)}, u32[]{:S(2)}) async-start(bf16[128,16,512]{0,2,1:T(8,128)(2,1)} %bitcast.6), calls=%async_computation | async-start | bytes 4194304 | tf_op jit(solution)/shard_map/all_to_all | solution.py:16
  19.1 4.1 %multiply_reduce_fusion.1 = f32[]{:T(128)} fusion(f32[512,2048]{1,0:T(8,128)} %param.7), kind=kLoop, calls=%fused_computation.4 | loop fusion | flops 2097151 | bytes 4194308 | tf_op jit(solution)/shard_map/reduce_sum | solution.py:26
  23.3 77.5 %all-to-all-done = bf16[128,16,512]{0,2,1:T(8,128)(2,1)S(1)} async-done(((bf16[128,16,512]{0,2,1:T(8,128)(2,1)}), bf16[128,16,512]{0,2,1:T(8,128)(2,1)S(1)}, u32[]{:S(2)}, u32[]{:S(2)}) %all-to-all-start) | async-done | bytes 2097184 | tf_op jit(solution)/shard_map/all_to_all | solution.py:16
  100.7 2.6 copy.10
  103.3 52.0 %all-gather.2.cloned.1.call-done = bf16[2048,2048]{1,0:T(8,128)(2,1)} async-done(((bf16[128,2048]{1,0:T(8,128)(2,1)}), bf16[2048,2048]{1,0:T(8,128)(2,1)}) %all-gather.2.cloned.1.call-update) | async-done | bytes 8388624 | tf_op jit(solution)/shard_map/all_gather | solution.py:19
  155.4 0.0 copy-start.2
  155.4 0.0 copy-start.3
  155.4 10.9 %fusion.1 = (f32[512]{0:T(512)S(1)}, f32[2048]{0:T(1024)S(1)}, f32[512,2048]{1,0:T(8,128)}) fusion(bf16[2048,512]{1,0:T(8,128)(2,1)} %bitcast.7, bf16[2048,2048]{1,0:T(8,128)(2,1)} %all-gather.2.cloned.1.call-done), kind=kOutput, calls=%fused_computation.6 | convolution fusion | flops 4299159040 | bytes 14690304 | tf_op jit(solution)/shard_map/dot_general | solution.py:17
  166.3 30.4 %psum.30 = f32[2048]{0:T(1024)S(1)} all-reduce(f32[2048]{0:T(1024)S(1)} %get-tuple-element.5), channel_id=1, replica_groups=mesh['row'=16,'col'=2] {'row'}, use_global_device_ids=true, to_apply=%region_5.0 | all-reduce | flops 2048 | bytes 16384 | tf_op jit(solution)/shard_map/psum | solution.py:28
  196.7 2.5 psum.29
  199.2 0.0 copy-done.2
  199.2 0.0 copy-done.3
  199.2 0.0 copy-start
  199.2 0.0 copy-start.1
  199.2 4.1 %multiply_reduce_fusion = f32[]{:T(128)} fusion(f32[512,2048]{1,0:T(8,128)} %get-tuple-element.10, f32[2048]{0:T(1024)S(1)} %multiply_add_fusion.1, f32[512]{0:T(512)S(1)} %multiply_add_fusion.2), kind=kLoop, calls=%fused_computation.1 | loop fusion | flops 4194303 | bytes 4204548 | tf_op jit(solution)/shard_map/reduce_sum | solution.py:33
  203.3 49.3 %all-reduce = (f32[]{:T(128)}, f32[]{:T(128)}) all-reduce(f32[]{:T(128)} %multiply_reduce_fusion, f32[]{:T(128)} %multiply_reduce_fusion.1), channel_id=1, replica_groups=mesh['row'=16,'col'=2] {'row','col'}, use_global_device_ids=true, to_apply=%region_7.0 | all-reduce | flops 2 | bytes 16 | tf_op jit(solution)/shard_map/psum | solution.py:33
  253.9 8.9 %multiply_subtract_fusion = (f32[512,2048]{1,0:T(8,128)}, f32[512,2048]{1,0:T(8,128)}) fusion(f32[512,2048]{1,0:T(8,128)} %param.7, f32[]{:T(128)S(6)} %mul_shard_map.3, f32[]{:T(128)S(6)} %max_shard_map.3, f32[512,2048]{1,0:T(8,128)} %get-tuple-element.10, f32[2048]{0:T(1024)S(1)} %multiply_add_fusion.1, f32[512]{0:T(512)S(1)} %multiply_add_fusion.2), kind=kLoop, calls=%fused_computation | loop fusion | flops 5242880 | bytes 16787464 | tf_op jit(solution)/shard_map/sub | solution.py:38
  262.9 0.0 copy-done
  262.9 0.0 copy-done.1
  (2 shorter events, 0.0 us)
Async XLA Ops:
  7.2 148.2 %all-gather.2.cloned.1.call-start = ((), (), s32[]{:S(2)}) async-start(), calls=%async_computation.1 | async-start | bytes 8912896 | tf_op jit(solution)/shard_map/all_gather | solution.py:19
  12.0 88.8 %all-to-all-start = ((bf16[128,16,512]{0,2,1:T(8,128)(2,1)}), bf16[128,16,512]{0,2,1:T(8,128)(2,1)S(1)}, u32[]{:S(2)}, u32[]{:S(2)}) async-start(bf16[128,16,512]{0,2,1:T(8,128)(2,1)} %bitcast.6), calls=%async_computation | async-start | bytes 4194304 | tf_op jit(solution)/shard_map/all_to_all | solution.py:16
  155.4 43.8 %copy-start.2 = (f32[2048]{0:T(1024)S(1)}, f32[2048]{0:T(1024)}, u32[]{:S(2)}) copy-start(f32[2048]{0:T(1024)} %param.9) | copy-start | bytes 24580
  155.4 43.8 %copy-start.3 = (f32[512]{0:T(512)S(1)}, f32[512]{0:T(512)}, u32[]{:S(2)}) copy-start(f32[512]{0:T(512)} %param.8) | copy-start | bytes 6148
  199.2 63.7 %copy-start = (f32[2048]{0:T(1024)}, f32[2048]{0:T(1024)S(1)}, u32[]{:S(2)}) copy-start(f32[2048]{0:T(1024)S(1)} %multiply_add_fusion.1) | copy-start | bytes 24580
  199.2 63.6 %copy-start.1 = (f32[512]{0:T(512)}, f32[512]{0:T(512)S(1)}, u32[]{:S(2)}) copy-start(f32[512]{0:T(512)S(1)} %multiply_add_fusion.2) | copy-start | bytes 6148
Sparse Core Ops, SparseCore 0:
  10.7 144.5 all-gather.1
where the time goes:
time: 270 us
  waiting for transfers between devices  130 us (48%)
  blocking collectives  82.2 us (30%)
  other arithmetic  17.1 us (6%)
  between operations  15.4 us (6%)
  matrix products  10.9 us (4%)
  starting transfers between devices  7.21 us (3%)
  local copies, waits for them, and re-layouts  6.67 us (2%)
    all_to_all x1, waiting for transfers between devices, per_device(): lax.all_to_all(acts, 'row', split_axis=1, concat_axis=0, tiled=True)  77.5 us
    all_gather x1, waiting for transfers between devices, per_device(): lax.all_gather(out_grads, 'row', axis=0, tiled=True)  52 us
    psum x1, blocking collectives, per_device(): update_total = lax.psum(jnp.sum(unclipped * unclipped), ('row', 'col'))  49.3 us
    psum x1, blocking collectives, per_device(): col_total = lax.psum(col_squares, 'row')  30.4 us
    dot_general x1, matrix products, per_device(): lax.dot_general(columns, lax.all_gather(out_grads, 'row', axis=0, tiled=T...  10.9 us
    sub x1, other arithmetic, per_device(): new_weight = weight - step_size * update  8.93 us
    all_to_all x1, starting transfers between devices, per_device(): lax.all_to_all(acts, 'row', split_axis=1, concat_axis=0, tiled=True)  7.17 us
  transfers between devices with their start and end apart: 2, of which 2 were waited for; matrix products, arithmetic and copies ran while one was open for 4% of the time, Pallas kernels for 0%

commit v1 on v0

--- a/solution.py
+++ b/solution.py
@@ -8,6 +8,27 @@
 relative_rate = 0.05
 
 
+def joined_along(blocks, dim):
+    lengths = list(blocks.shape[1:])
+    lengths[dim] *= blocks.shape[0]
+    return jnp.moveaxis(blocks, 0, dim).reshape(lengths)
+
+
+def collected_by_bits(array, axis):
+    size, index = (lax.axis_size(axis), lax.axis_index(axis))
+    pieces, stride = (array[None], 1)
+    while stride < size:
+        theirs = lax.ppermute(pieces, axis, [(i, i ^ stride) for i in range(size)])
+        low = index & stride == 0
+        pieces = jnp.concatenate([jnp.where(low, pieces, theirs), jnp.where(low, theirs, pieces)])
+        stride *= 2
+    return pieces
+
+
+def gather_by_bits(shard, axis, dim):
+    return joined_along(collected_by_bits(shard, axis), dim)
+
+
 def per_device(acts, out_grads, weight, row_state, col_state):
     n_col = lax.axis_size("col")
     width = acts.shape[1]
@@ -16,7 +37,7 @@
     columns = lax.all_to_all(acts, "row", split_axis=1, concat_axis=0, tiled=True)
     gradient = lax.dot_general(
         columns,
-        lax.all_gather(out_grads, "row", axis=0, tiled=True),
+        gather_by_bits(out_grads, "row", 0),
         (((0,), (0,)), ((), ())),
         preferred_element_type=jnp.float32,
     )

time: 270 us -> 439 us (1.63)
  waiting for transfers between devices: 130 us -> 282 us
  local copies, waits for them, and re-layouts: 6.67 us -> 26.4 us
  between operations: 15.4 us -> 2.15 us
  other arithmetic: 17.1 us -> 24.8 us
    ppermute x0 -> x4, waiting for transfers between devices: none -> 264 us  [collected_by_bits(): theirs = lax.ppermute(pieces, axis, [(i, i ^ stride) for i in range(size)])]
    all_to_all x1, waiting for transfers between devices: 77.5 us -> 18 us  [per_device(): lax.all_to_all(acts, 'row', split_axis=1, concat_axis=0, tiled=True)]
    all_gather x1 -> x0, waiting for transfers between devices: 52 us -> none  [per_device(): lax.all_gather(out_grads, 'row', axis=0, tiled=True)]
    unnamed x9 -> x19, local copies, waits for them, and re-layouts: 4.09 us -> 22.4 us
    select_n x0 -> x4, other arithmetic: none -> 7.54 us  [collected_by_bits(): jnp.where(low, pieces, theirs)]
    ppermute x0 -> x4, starting transfers between devices: none -> 5.23 us  [collected_by_bits(): theirs = lax.ppermute(pieces, axis, [(i, i ^ stride) for i in range(size)])]
  transfers between devices with their start and end apart: 2 -> 5, of which waited for: 2 -> 5; matrix products, arithmetic and copies ran while one was open for 4% -> 4% of each run, Pallas kernels for 0% -> 0%
where the time goes in v1:
time: 439 us
  waiting for transfers between devices  282 us (64%)
  blocking collectives  84.3 us (19%)
  local copies, waits for them, and re-layouts  26.4 us (6%)
  other arithmetic  24.8 us (6%)
  starting transfers between devices  10.4 us (2%)
  matrix products  8.94 us (2%)
    ppermute x4, waiting for transfers between devices, collected_by_bits(): theirs = lax.ppermute(pieces, axis, [(i, i ^ stride) for i in range(size)])  264 us
    psum x1, blocking collectives, per_device(): update_total = lax.psum(jnp.sum(unclipped * unclipped), ('row', 'col'))  49.4 us
    psum x1, blocking collectives, per_device(): col_total = lax.psum(col_squares, 'row')  32.4 us
    unnamed x19, local copies, waits for them, and re-layouts  22.4 us
    all_to_all x1, waiting for transfers between devices, per_device(): lax.all_to_all(acts, 'row', split_axis=1, concat_axis=0, tiled=True)  18 us
    dot_general x1, matrix products, per_device(): lax.dot_general(columns, gather_by_bits(out_grads, 'row', 0), (((0,), (0,...  8.94 us
  transfers between devices with their start and end apart: 5, of which 5 were waited for; matrix products, arithmetic and copies ran while one was open for 4% of the time, Pallas kernels for 0%

profile of v1, /device:TPU:12, one launch (start us, length us, event | category | flops | bytes accessed | tf_op | source)
XLA Modules:
  0.0 438.6 jit_solution(15380795235197888577)
XLA Ops:
  0.6 1.3 copy.13
  1.9 1.6 collective-permute-start
  3.5 12.2 %collective-permute-done = bf16[1,128,2048]{1,2,0:T(8,128)(2,1)S(1)} collective-permute-done((bf16[1,128,2048]{1,2,0:T(8,128)(2,1)S(1)}, bf16[1,128,2048]{1,2,0:T(8,128)(2,1)S(1)}, u32[]{:S(2)}, u32[]{:S(2)}) %collective-permute-start) | collective-permute-done | bytes 524320 | tf_op jit(solution)/shard_map/ppermute | solution.py:21
  16.4 23.5 %collective-permute-done.1 = bf16[2,128,2048]{1,2,0:T(8,128)(2,1)S(1)} collective-permute-done((bf16[2,128,2048]{1,2,0:T(8,128)(2,1)S(1)}, bf16[2,128,2048]{1,2,0:T(8,128)(2,1)S(1)}, u32[]{:S(2)}, u32[]{:S(2)}) %collective-permute-start.1) | collective-permute-done | bytes 1048608 | tf_op jit(solution)/shard_map/ppermute | solution.py:21
  41.8 45.3 %collective-permute-done.2 = bf16[4,128,2048]{1,2,0:T(8,128)(2,1)} collective-permute-done((bf16[4,128,2048]{1,2,0:T(8,128)(2,1)S(1)}, bf16[4,128,2048]{1,2,0:T(8,128)(2,1)}, u32[]{:S(2)}, u32[]{:S(2)}) %collective-permute-start.2) | collective-permute-done | bytes 2097184 | tf_op jit(solution)/shard_map/ppermute | solution.py:21
  87.1 2.1 broadcast_select_fusion.3
  89.2 2.6 pad_maximum_fusion
  91.9 2.6 collective-permute-start.3
  94.5 4.1 copy.14
  98.5 3.9 copy.15
  102.5 5.1 %all-to-all-start = ((bf16[128,16,512]{2,0,1:T(8,128)(2,1)}), bf16[128,16,512]{2,0,1:T(8,128)(2,1)}, u32[]{:S(2)}, u32[]{:S(2)}) async-start(bf16[128,16,512]{2,0,1:T(8,128)(2,1)} %copy.15), calls=%async_computation | async-start | bytes 4194304 | tf_op jit(solution)/shard_map/all_to_all | solution.py:37
  107.6 4.1 multiply_reduce_fusion.1
  111.7 182.7 %collective-permute-done.3 = bf16[8,128,2048]{1,2,0:T(8,128)(2,1)} collective-permute-done((bf16[8,128,2048]{1,2,0:T(8,128)(2,1)}, bf16[8,128,2048]{1,2,0:T(8,128)(2,1)}, u32[]{:S(2)}, u32[]{:S(2)}) %collective-permute-start.3) | collective-permute-done | bytes 4194336 | tf_op jit(solution)/shard_map/ppermute | solution.py:21
  294.4 5.2 %broadcast_select_fusion.1 = (bf16[8,128,2048]{1,2,0:T(8,128)(2,1)}, bf16[8,128,2048]{1,2,0:T(8,128)(2,1)}) fusion(bf16[8,128,2048]{1,2,0:T(8,128)(2,1)} %collective-permute-done.3, pred[]{:T(512)S(6)} %eq.12, bf16[4,128,2048]{1,2,0:T(8,128)(2,1)S(1)} %copy-done.1, bf16[4,128,2048]{1,2,0:T(8,128)(2,1)S(1)} %get-tuple-element.20), kind=kLoop, calls=%fused_computation.12 | loop fusion | flops 6291456 | bytes 16777216 | tf_op jit(solution)/shard_map/jit(_where)/select_n | solution.py:23
  299.6 18.0 %all-to-all-done = bf16[128,16,512]{2,0,1:T(8,128)(2,1)} async-done(((bf16[128,16,512]{2,0,1:T(8,128)(2,1)}), bf16[128,16,512]{2,0,1:T(8,128)(2,1)}, u32[]{:S(2)}, u32[]{:S(2)}) %all-to-all-start) | async-done | bytes 2097184 | tf_op jit(solution)/shard_map/all_to_all | solution.py:37
  317.6 8.9 %fusion.6 = (f32[512]{0:T(512)S(1)}, f32[2048]{0:T(1024)S(1)}, f32[2048,512,1]{1,0,2:T(8,128)}) fusion(bf16[128,16,512]{2,0,1:T(8,128)(2,1)} %all-to-all-done, bf16[8,128,2048]{1,2,0:T(8,128)(2,1)} %get-tuple-element.19, bf16[8,128,2048]{1,2,0:T(8,128)(2,1)} %get-tuple-element.18), kind=kOutput, calls=%fused_computation.14 | convolution fusion | flops 4303353344 | bytes 14690304 | tf_op jit(solution)/shard_map/dot_general | solution.py:38
  326.5 32.4 %psum.30 = f32[2048]{0:T(1024)S(1)} all-reduce(f32[2048]{0:T(1024)S(1)} %get-tuple-element.13), channel_id=1, replica_groups=mesh['row'=16,'col'=2] {'row'}, use_global_device_ids=true, to_apply=%region_5.6 | all-reduce | flops 2048 | bytes 16384 | tf_op jit(solution)/shard_map/psum | solution.py:49
  358.9 2.5 psum.29
  361.4 4.2 multiply_reduce_fusion
  365.6 5.3 %copy.16 = f32[512,2048]{0,1:T(8,128)} copy(f32[512,2048]{1,0:T(8,128)} %param.7) | data formatting | bytes 8388608 | tf_op args[2]
  371.0 49.4 %all-reduce = (f32[]{:T(128)}, f32[]{:T(128)}) all-reduce(f32[]{:T(128)} %multiply_reduce_fusion, f32[]{:T(128)} %multiply_reduce_fusion.1), channel_id=1, replica_groups=mesh['row'=16,'col'=2] {'row','col'}, use_global_device_ids=true, to_apply=%region_7.8 | all-reduce | flops 2 | bytes 16 | tf_op jit(solution)/shard_map/psum | solution.py:54
  421.8 6.1 %multiply_subtract_fusion = (f32[512,2048]{0,1:T(8,128)}, f32[512,2048]{0,1:T(8,128)}) fusion(f32[512,2048]{0,1:T(8,128)} %copy.16, f32[]{:T(128)S(6)} %mul_shard_map.3, f32[]{:T(128)S(6)} %max_shard_map.3, f32[2048]{0:T(1024)S(1)} %multiply_add_fusion, f32[512]{0:T(512)S(1)} %multiply_add_fusion.1, f32[2048,512,1]{1,0,2:T(8,128)} %get-tuple-element.26), kind=kLoop, calls=%fused_computation.8 | loop fusion | flops 5242880 | bytes 16787464 | tf_op jit(solution)/shard_map/sub | solution.py:59
  427.9 5.3 %copy.17 = f32[512,2048]{1,0:T(8,128)} copy(f32[512,2048]{0,1:T(8,128)} %get-tuple-element.16) | data formatting | bytes 8388608
  433.2 5.3 %copy.18 = f32[512,2048]{1,0:T(8,128)} copy(f32[512,2048]{0,1:T(8,128)} %get-tuple-element.17) | data formatting | bytes 8388608
  (22 shorter events, 2.6 us)
Async XLA Ops:
  1.9 13.7 %collective-permute-start = (bf16[1,128,2048]{1,2,0:T(8,128)(2,1)S(1)}, bf16[1,128,2048]{1,2,0:T(8,128)(2,1)S(1)}, u32[]{:S(2)}, u32[]{:S(2)}) collective-permute-start(bf16[1,128,2048]{1,2,0:T(8,128)(2,1)S(1)} %bitcast.26), channel_id=1, source_target_pairs={{0,2},{2,0},{4,6},{6,4},{8,10},{10,8},{12,14},{14,12},{16,18},{18,... | collective-permute-start | bytes 1572872 | tf_op jit(solution)/shard_map/ppermute | solution.py:21
  15.9 24.1 %collective-permute-start.1 = (bf16[2,128,2048]{1,2,0:T(8,128)(2,1)S(1)}, bf16[2,128,2048]{1,2,0:T(8,128)(2,1)S(1)}, u32[]{:S(2)}, u32[]{:S(2)}) collective-permute-start(bf16[2,128,2048]{1,2,0:T(8,128)(2,1)S(1)} %pad_maximum_fusion.2), channel_id=1, source_target_pairs={{0,4},{2,6},{4,0},{6,2},{8,12},{10,14},{12,8},{14,10},{16,20},{18,... | collective-permute-start | bytes 3145736 | tf_op jit(solution)/shard_map/ppermute | solution.py:21
  40.1 1.0 copy-start.2
  41.3 45.8 %collective-permute-start.2 = (bf16[4,128,2048]{1,2,0:T(8,128)(2,1)S(1)}, bf16[4,128,2048]{1,2,0:T(8,128)(2,1)}, u32[]{:S(2)}, u32[]{:S(2)}) collective-permute-start(bf16[4,128,2048]{1,2,0:T(8,128)(2,1)S(1)} %pad_maximum_fusion.1), channel_id=1, source_target_pairs={{0,8},{2,10},{4,12},{6,14},{8,0},{10,2},{12,4},{14,6},{16,24},{18,... | collective-permute-start | bytes 6291464 | tf_op jit(solution)/shard_map/ppermute | solution.py:21
  89.2 2.7 copy-start
  91.9 202.5 %collective-permute-start.3 = (bf16[8,128,2048]{1,2,0:T(8,128)(2,1)}, bf16[8,128,2048]{1,2,0:T(8,128)(2,1)}, u32[]{:S(2)}, u32[]{:S(2)}) collective-permute-start(bf16[8,128,2048]{1,2,0:T(8,128)(2,1)} %pad_maximum_fusion), channel_id=1, source_target_pairs={{0,16},{2,18},{4,20},{6,22},{8,24},{10,26},{12,28},{14,30},{16,0},... | collective-permute-start | bytes 12582920 | tf_op jit(solution)/shard_map/ppermute | solution.py:21
  102.5 215.1 %all-to-all-start = ((bf16[128,16,512]{2,0,1:T(8,128)(2,1)}), bf16[128,16,512]{2,0,1:T(8,128)(2,1)}, u32[]{:S(2)}, u32[]{:S(2)}) async-start(bf16[128,16,512]{2,0,1:T(8,128)(2,1)} %copy.15), calls=%async_computation | async-start | bytes 4194304 | tf_op jit(solution)/shard_map/all_to_all | solution.py:37
  107.6 186.8 %copy-start.1 = (bf16[4,128,2048]{1,2,0:T(8,128)(2,1)S(1)}, bf16[4,128,2048]{1,2,0:T(8,128)(2,1)}, u32[]{:S(2)}) copy-start(bf16[4,128,2048]{1,2,0:T(8,128)(2,1)} %copy-done) | copy-start | bytes 6291460
  317.6 43.8 %copy-start.5 = (f32[2048]{0:T(1024)S(1)}, f32[2048]{0:T(1024)}, u32[]{:S(2)}) copy-start(f32[2048]{0:T(1024)} %param.9) | copy-start | bytes 24580
  317.6 43.8 %copy-start.6 = (f32[512]{0:T(512)S(1)}, f32[512]{0:T(512)}, u32[]{:S(2)}) copy-start(f32[512]{0:T(512)} %param.8) | copy-start | bytes 6148
  361.4 60.4 %copy-start.3 = (f32[2048]{0:T(1024)}, f32[2048]{0:T(1024)S(1)}, u32[]{:S(2)}) copy-start(f32[2048]{0:T(1024)S(1)} %multiply_add_fusion) | copy-start | bytes 24580
  361.4 60.4 %copy-start.4 = (f32[512]{0:T(512)}, f32[512]{0:T(512)S(1)}, u32[]{:S(2)}) copy-start(f32[512]{0:T(512)S(1)} %multiply_add_fusion.1) | copy-start | bytes 6148
